TPU v7x, 512 devices: a whole 4x4x16 slice. The times are simulated.
512 devices in a mesh: mem: 16 (over z), sp: 32 (over x, y, core).
Axes of the slice: x: 4, y: 4, z: 16, core: 2. Of those that a mesh axis runs over, the one named last changes fastest.
Arguments:
- ensemble: bfloat16 [256, 131072], P('mem', 'sp'), may hold values from -6 to 6
- predicted: bfloat16 [256, 65536], P('mem', 'sp'), may hold values from -2 to 2
- observed: float32 [65536], P('sp'), may hold values from -6 to 6
- perturbation: bfloat16 [256, 65536], P('mem', 'sp'), may hold values from -6 to 6
- noise_variance: float32 [512], P('sp'), may hold values from 0.25 to 4
- block_lists: int32 [32, 64], P('sp'), may hold values from 0 to 511, as said below
- localization: int32 [1024, 64], P('sp'), may hold values 0 or 1
Outputs:
- increment: float32 [256, 131072], P('mem', 'sp')
Inputs may be any that keep to these rules, and one draw needn't show every extreme that they name: `block_lists`: row t lists the 64 distinct data blocks used by the bricks of index t of sp, in increasing order; block j is held by index j // 16; a row uses 1 to 3 blocks of each holder, exactly 3 of some holder, and every holder gives 3 blocks to some row.
All inputs are finite; a program needn't handle non-finite values. No bound on the sum of `localization` on one device may be relied on, other than what follows from the above.
Results may differ from a plain program's by a relative error of at most 0.0055.
Values may be sent and summed in bfloat16 or wider, within the bound.
No kernel may reach another device: no remote copies, remote signals or barrier semaphores. Data moves between devices by JAX's collectives and lax.ppermute only.
A program may use at most 64 MiB of HBM per device.

v0:
```python
import jax
import jax.numpy as jnp
from jax import lax
from jax.sharding import PartitionSpec as P

SLOTS = 3
ENSEMBLE_SCALE = 2.0**13
PREDICTED_SCALE = 2.0**14


def per_device(
    ensemble, predicted, observed, perturbation, noise_variance, block_lists, localization
):
    bf16, f16, f32 = (jnp.bfloat16, jnp.float16, jnp.float32)
    mem, sp = (lax.axis_size("mem"), lax.axis_size("sp"))
    local = ensemble.shape[0]
    members = local * mem
    cells = ensemble.shape[1]
    bricks = localization.shape[0]
    brick = cells // bricks
    blocks = noise_variance.shape[0]
    data = predicted.shape[1]
    block = data // blocks
    need = block_lists.shape[1]
    needed = block_lists[0]
    holder = needed // blocks
    before = jnp.sum(needed[None, :] < (holder * blocks)[:, None], axis=1)
    slot = holder * SLOTS + (jnp.arange(need) - before)
    slot_hot = slot[:, None] == jnp.arange(sp * SLOTS)[None, :]
    asked = jnp.sum(jnp.where(slot_hot, (needed % blocks)[:, None], 0), axis=0)
    asked = jnp.pad(asked.reshape(sp, SLOTS), ((0, 0), (0, 128 - SLOTS)))
    wanted = lax.all_to_all(asked, "sp", split_axis=0, concat_axis=0, tiled=True)
    wanted = wanted[:, :SLOTS].reshape(-1)
    slot_pattern = jnp.dot(
        localization.astype(bf16), slot_hot.astype(bf16), preferred_element_type=f32
    ).astype(bf16)
    sent = jnp.concatenate(
        [
            (predicted.astype(f32) * PREDICTED_SCALE).astype(f16),
            (ensemble.astype(f32) * ENSEMBLE_SCALE).astype(f16),
        ],
        axis=1,
    )
    whole = lax.all_gather(sent, "mem", axis=0, tiled=True)
    whole_predicted = whole[:, :data].astype(f32)
    whole_ensemble = whole[:, data:].astype(f32)
    data_mean = jnp.sum(whole_predicted, axis=0) / members
    data_anomalies = (whole_predicted - data_mean).astype(bf16)
    variance = jnp.repeat(noise_variance, block)
    innovation = (
        observed[None, :] + jnp.sqrt(variance) * perturbation.astype(f32) - predicted.astype(f32)
    )
    weighted = (innovation / variance).astype(bf16)
    products = jnp.einsum(
        "njd,mjd->jnm",
        weighted.reshape(local, blocks, block),
        data_anomalies.reshape(members, blocks, block),
        preferred_element_type=f32,
    ).astype(bf16)
    picked = (wanted[:, None] == jnp.arange(blocks)[None, :]).astype(bf16)
    chosen = jnp.einsum("sj,jnm->snm", picked, products, preferred_element_type=f32).astype(bf16)
    chosen = chosen.reshape(sp, SLOTS * local, members)
    got = lax.all_to_all(chosen, "sp", split_axis=0, concat_axis=0, tiled=True)
    got = got.reshape(sp * SLOTS, local, members)
    gains = jnp.einsum("bs,snm->bnm", slot_pattern, got, preferred_element_type=f32).astype(bf16)
    model_mean = jnp.sum(whole_ensemble, axis=0) / members
    model_anomalies = (whole_ensemble - model_mean).astype(bf16)
    increment = jnp.einsum(
        "bnm,mbc->nbc",
        gains,
        model_anomalies.reshape(members, bricks, brick),
        preferred_element_type=f32,
    )
    return increment.reshape(local, cells) / ((members - 1) * (ENSEMBLE_SCALE * PREDICTED_SCALE))


def solution(mesh):
    in_specs = (
        P("mem", "sp"),
        P("mem", "sp"),
        P("sp"),
        P("mem", "sp"),
        P("sp"),
        P("sp", None),
        P("sp", None),
    )
    return jax.shard_map(
        per_device, mesh=mesh, in_specs=in_specs, out_specs=P("mem", "sp"), check_vma=False
    )
```

profile of v0, /device:TPU:1, one launch (start us, length us, event | category | flops | bytes accessed | tf_op | source)
XLA Modules:
  0.0 100.3 jit_solution(8255561236363733523)
XLA Ops:
  0.0 0.7 broadcast_multiply_fusion.2
  0.7 0.8 convert_reduce_fusion.2
  1.5 0.1 select_reduce_fusion
  1.6 0.1 reshape.108
  1.7 0.6 pad.4
  2.3 10.4 %all-to-all-start = ((s32[32,1,128]{2,1,0:T(1,128)}), s32[32,1,128]{2,1,0:T(1,128)S(1)}, u32[]{:S(2)}, u32[]{:S(2)}) async-start(s32[32,1,128]{2,1,0:T(1,128)} %bitcast.3), calls=%async_computation | async-start | bytes 32768 | tf_op jit(solution)/shard_map/all_to_all | solution.py:32
  12.7 0.7 bitcast_sqrt_fusion
  13.4 0.7 broadcast_bitcast_fusion
  14.2 0.9 multiply_convert_fusion
  15.1 0.9 fusion.24
  16.0 0.1 pad_maximum_fusion
  16.1 50.7 %all-gather.1 = f16[256,6144]{1,0:T(8,128)(2,1)S(1)} all-gather(f16[16,6144]{1,0:T(8,128)(2,1)S(1)} %pad_maximum_fusion), channel_id=1, replica_groups=mesh['mem'=16,'sp'=32] {'mem'}, dimensions={0}, use_global_device_ids=true | all-gather | bytes 3342336 | tf_op jit(solution)/shard_map/all_gather | solution.py:44
  66.8 0.2 convert_reduce_fusion.1
  67.0 0.4 convolution_convert_fusion.2
  67.3 0.0 all-to-all-done
  67.4 0.1 eq.33
  67.5 0.4 convolution_convert_fusion
  67.9 1.3 %copy.33 = bf16[96,16,256]{2,1,0:T(8,128)(2,1)} copy(bf16[96,16,256]{2,0,1:T(8,128)(2,1)S(1)} %convolution_convert_fusion) | data formatting | bytes 1572864 | tf_op jit(solution)/shard_map/convert_element_type | solution.py:61
  69.2 13.9 %all-to-all-start.1 = ((bf16[32,48,256]{2,1,0:T(8,128)(2,1)}), bf16[32,48,256]{2,1,0:T(8,128)(2,1)}, u32[]{:S(2)}, u32[]{:S(2)}) async-start(bf16[32,48,256]{2,1,0:T(8,128)(2,1)} %bitcast.54), calls=%async_computation.1 | async-start | bytes 1572864 | tf_op jit(solution)/shard_map/all_to_all | solution.py:63
  83.1 0.3 convert_reduce_fusion
  83.4 14.0 %all-to-all-done.1 = bf16[32,48,256]{2,1,0:T(8,128)(2,1)} async-done(((bf16[32,48,256]{2,1,0:T(8,128)(2,1)}), bf16[32,48,256]{2,1,0:T(8,128)(2,1)}, u32[]{:S(2)}, u32[]{:S(2)}) %all-to-all-start.1) | async-done | bytes 786464 | tf_op jit(solution)/shard_map/all_to_all | solution.py:63
  97.4 1.6 %convolution_convert_fusion.1 = bf16[32,16,256]{2,0,1:T(8,128)(2,1)S(1)} fusion(bf16[96,16,256]{2,1,0:T(8,128)(2,1)} %bitcast.8, s32[64]{0:T(128)S(1)} %subtract_add_fusion, s32[32,64]{1,0:T(8,128)S(1)} %copy-done), kind=kOutput, calls=%fused_computation.11 | convolution fusion | flops 25701376 | bytes 1057024 | tf_op jit(solution)/shard_map/bs,snm->bnm/dot_general | solution.py:65
  99.0 0.6 fusion.9
  99.5 0.7 copy.65
  (5 shorter events, 0.0 us)
Async XLA Ops:
  2.3 65.0 %all-to-all-start = ((s32[32,1,128]{2,1,0:T(1,128)}), s32[32,1,128]{2,1,0:T(1,128)S(1)}, u32[]{:S(2)}, u32[]{:S(2)}) async-start(s32[32,1,128]{2,1,0:T(1,128)} %bitcast.3), calls=%async_computation | async-start | bytes 32768 | tf_op jit(solution)/shard_map/all_to_all | solution.py:32
  67.3 30.0 %copy-start = (s32[32,64]{1,0:T(8,128)S(1)}, s32[32,64]{1,0:T(8,128)}, u32[]{:S(2)}) copy-start(s32[32,64]{1,0:T(8,128)} %param.13) | copy-start | bytes 24580
  69.2 28.2 %all-to-all-start.1 = ((bf16[32,48,256]{2,1,0:T(8,128)(2,1)}), bf16[32,48,256]{2,1,0:T(8,128)(2,1)}, u32[]{:S(2)}, u32[]{:S(2)}) async-start(bf16[32,48,256]{2,1,0:T(8,128)(2,1)} %bitcast.54), calls=%async_computation.1 | async-start | bytes 1572864 | tf_op jit(solution)/shard_map/all_to_all | solution.py:63
where the time goes:
time: 101 us; the launch traced here: 100 us
  blocking collectives  50.7 us (50%)
  starting transfers between devices  24.2 us (24%)
  waiting for transfers between devices  14 us (14%)
  local copies, waits for them, and re-layouts  4.36 us (4%)
  other arithmetic  4 us (4%)
  matrix products  2.93 us (3%)
    all_gather x1, blocking collectives, per_device(): whole = lax.all_gather(sent, 'mem', axis=0, tiled=True)  50.7 us
    all_to_all x1, waiting for transfers between devices, per_device(): got = lax.all_to_all(chosen, 'sp', split_axis=0, concat_axis=0, tiled=True)  14 us
    all_to_all x1, starting transfers between devices, per_device(): got = lax.all_to_all(chosen, 'sp', split_axis=0, concat_axis=0, tiled=True)  13.9 us
    all_to_all x1, starting transfers between devices, per_device(): lax.all_to_all(asked, 'sp', split_axis=0, concat_axis=0, tiled=True)  10.4 us
  transfers between devices with their start and end apart: 2, of which 1 were waited for; matrix products, arithmetic and copies ran while one was open for 4% of the time, Pallas kernels for 0%

commit v1 on v0

--- a/solution.py
+++ b/solution.py
@@ -41,7 +41,19 @@
         ],
         axis=1,
     )
-    whole = lax.all_gather(sent, "mem", axis=0, tiled=True)
+    ways, here, lap = (lax.axis_size("mem"), lax.axis_index("mem"), sent.shape[0])
+    shape = [n * ways if d == 0 else n for d, n in enumerate(sent.shape)]
+    full = lax.dynamic_update_slice_in_dim(jnp.zeros(shape, sent.dtype), sent, here * lap, axis=0)
+    going_up = going_down = sent
+    for far in range(1, ways // 2 + 1):
+        going_up = lax.ppermute(going_up, "mem", [(d, (d + 1) % ways) for d in range(ways)])
+        full = lax.dynamic_update_slice_in_dim(full, going_up, (here - far) % ways * lap, axis=0)
+        if 2 * far < ways:
+            going_down = lax.ppermute(going_down, "mem", [(d, (d - 1) % ways) for d in range(ways)])
+            full = lax.dynamic_update_slice_in_dim(
+                full, going_down, (here + far) % ways * lap, axis=0
+            )
+    whole = full
     whole_predicted = whole[:, :data].astype(f32)
     whole_ensemble = whole[:, data:].astype(f32)
     data_mean = jnp.sum(whole_predicted, axis=0) / members

time: 101 us -> 429 us (4.25); the launches traced: 100 us -> 423 us
  local copies, waits for them, and re-layouts: 4.36 us -> 311 us
  starting transfers between devices: 24.2 us -> 78.7 us
  blocking collectives: 50.7 us -> 0 us
  waiting for transfers between devices: 14 us -> 21.5 us
    dynamic_update_slice x0 -> x16, local copies, waits for them, and re-layouts: none -> 264 us  [the longest x8 131 us: per_device(): lax.dynamic_update_slice_in_dim(full, going_up, (here - far) % ways * lap...]
    ppermute x0 -> x15, starting transfers between devices: none -> 54.7 us  [the longest x7 36.9 us: per_device(): lax.ppermute(going_down, 'mem', [(d, (d - 1) % ways) for d in range(ways)])]
    all_gather x1 -> x0, blocking collectives: 50.7 us -> none  [per_device(): whole = lax.all_gather(sent, 'mem', axis=0, tiled=True)]
    ppermute x0 -> x15, local copies, waits for them, and re-layouts: none -> 40.9 us  [the longest x8 21.4 us: per_device(): lax.ppermute(going_up, 'mem', [(d, (d + 1) % ways) for d in range(ways)])]
    ppermute x0 -> x15, waiting for transfers between devices: none -> 8.98 us  [the longest x8 8.96 us: per_device(): lax.ppermute(going_up, 'mem', [(d, (d + 1) % ways) for d in range(ways)])]
    all_to_all x1, starting transfers between devices: 13.9 us -> 7.43 us  [per_device(): got = lax.all_to_all(chosen, 'sp', split_axis=0, concat_axis=0, tiled=True)]
    all_to_all x1, starting transfers between devices: 10.4 us -> 16.6 us  [per_device(): lax.all_to_all(asked, 'sp', split_axis=0, concat_axis=0, tiled=True)]
  transfers between devices with their start and end apart: 2 -> 17, of which waited for: 1 -> 8; matrix products, arithmetic and copies ran while one was open for 4% -> 70% of each run, Pallas kernels for 0% -> 0%
where the time goes in v1:
time: 429 us; the launch traced here: 423 us
  local copies, waits for them, and re-layouts  311 us (72%)
  starting transfers between devices  78.7 us (18%)
  waiting for transfers between devices  21.5 us (5%)
  other arithmetic  6.51 us (2%)
  matrix products  4.49 us (1%)
    dynamic_update_slice x8, local copies, waits for them, and re-layouts, per_device(): lax.dynamic_update_slice_in_dim(full, going_up, (here - far) % ways * lap...  131 us
    dynamic_update_slice x7, local copies, waits for them, and re-layouts, per_device(): lax.dynamic_update_slice_in_dim(full, going_down, (here + far) % ways * l...  119 us
    ppermute x7, starting transfers between devices, per_device(): lax.ppermute(going_down, 'mem', [(d, (d - 1) % ways) for d in range(ways)])  36.9 us
    ppermute x8, local copies, waits for them, and re-layouts, per_device(): lax.ppermute(going_up, 'mem', [(d, (d + 1) % ways) for d in range(ways)])  21.4 us
    ppermute x7, local copies, waits for them, and re-layouts, per_device(): lax.ppermute(going_down, 'mem', [(d, (d - 1) % ways) for d in range(ways)])  19.5 us
    ppermute x8, starting transfers between devices, per_device(): lax.ppermute(going_up, 'mem', [(d, (d + 1) % ways) for d in range(ways)])  17.7 us
    all_to_all x1, starting transfers between devices, per_device(): lax.all_to_all(asked, 'sp', split_axis=0, concat_axis=0, tiled=True)  16.6 us
    dynamic_update_slice x1, local copies, waits for them, and re-layouts, per_device(): lax.dynamic_update_slice_in_dim(jnp.zeros(shape, sent.dtype), sent, here...  14.3 us
  transfers between devices with their start and end apart: 17, of which 8 were waited for; matrix products, arithmetic and copies ran while one was open for 70% of the time, Pallas kernels for 0%

profile of v1, /device:TPU:1, one launch (start us, length us, event | category | flops | bytes accessed | tf_op | source)
XLA Modules:
  0.0 423.1 jit_solution(16193573151290321955)
XLA Ops:
  7.8 9.5 %collective-permute-start.1 = (f16[16,6144]{1,0:T(8,128)(2,1)S(1)}, f16[16,6144]{1,0:T(8,128)(2,1)S(1)}, u32[]{:S(2)}, u32[]{:S(2)}) collective-permute-start(f16[16,6144]{1,0:T(8,128)(2,1)S(1)} %pad_maximum_fusion), channel_id=1, source_target_pairs={{0,480},{32,0},{64,32},{96,64},{128,96},{160,128},{192,160},{224,1... | collective-permute-start | bytes 589832 | tf_op jit(solution)/shard_map/ppermute | solution.py:52
  21.9 4.6 %collective-permute-start.3 = (f16[16,6144]{1,0:T(8,128)(2,1)S(1)}, f16[16,6144]{1,0:T(8,128)(2,1)S(1)}, u32[]{:S(2)}, u32[]{:S(2)}) collective-permute-start(f16[16,6144]{1,0:T(8,128)(2,1)S(1)} %collective-permute-done.1), channel_id=1, source_target_pairs={{0,480},{32,0},{64,32},{96,64},{128,96},{160,128},{192,160},{224,1... | collective-permute-start | bytes 589832 | tf_op jit(solution)/shard_map/ppermute | solution.py:52
  30.2 4.6 %collective-permute-start.5 = (f16[16,6144]{1,0:T(8,128)(2,1)S(1)}, f16[16,6144]{1,0:T(8,128)(2,1)S(1)}, u32[]{:S(2)}, u32[]{:S(2)}) collective-permute-start(f16[16,6144]{1,0:T(8,128)(2,1)S(1)} %collective-permute-done.3), channel_id=1, source_target_pairs={{0,480},{32,0},{64,32},{96,64},{128,96},{160,128},{192,160},{224,1... | collective-permute-start | bytes 589832 | tf_op jit(solution)/shard_map/ppermute | solution.py:52
  53.0 4.6 %collective-permute-start.11 = (f16[16,6144]{1,0:T(8,128)(2,1)S(1)}, f16[16,6144]{1,0:T(8,128)(2,1)}, u32[]{:S(2)}, u32[]{:S(2)}) collective-permute-start(f16[16,6144]{1,0:T(8,128)(2,1)S(1)} %collective-permute-done.9), channel_id=1, source_target_pairs={{0,480},{32,0},{64,32},{96,64},{128,96},{160,128},{192,160},{224,1... | collective-permute-start | bytes 589832 | tf_op jit(solution)/shard_map/ppermute | solution.py:52
  62.1 4.6 %collective-permute-start.13 = (f16[16,6144]{1,0:T(8,128)(2,1)}, f16[16,6144]{1,0:T(8,128)(2,1)}, u32[]{:S(2)}, u32[]{:S(2)}) collective-permute-start(f16[16,6144]{1,0:T(8,128)(2,1)} %collective-permute-done.11), channel_id=1, source_target_pairs={{0,480},{32,0},{64,32},{96,64},{128,96},{160,128},{192,160},{224,1... | collective-permute-start | bytes 589832 | tf_op jit(solution)/shard_map/ppermute | solution.py:52
  69.6 16.6 %all-to-all-start = ((s32[32,1,128]{2,1,0:T(1,128)}), s32[32,1,128]{2,1,0:T(1,128)S(1)}, u32[]{:S(2)}, u32[]{:S(2)}) async-start(s32[32,1,128]{2,1,0:T(1,128)} %bitcast.4), calls=%async_computation | async-start | bytes 32768 | tf_op jit(solution)/shard_map/all_to_all | solution.py:32
  88.5 14.3 %dynamic_update_slice.48 = f16[256,6144]{0,1:T(8,128)(2,1)S(1)} dynamic-update-slice(f16[256,6144]{0,1:T(8,128)(2,1)S(1)} %broadcast_in_dim.16, f16[16,6144]{0,1:T(8,128)(2,1)} %copy.66, s32[]{:T(128)S(6)} %select_n.137, s32[]{:T(128)} %constant.124.clone.1) | dynamic-update-slice | bytes 393220 | tf_op jit(solution)/shard_map/dynamic_update_slice | solution.py:46
  105.7 16.7 %dynamic_update_slice.49 = f16[256,6144]{0,1:T(8,128)(2,1)S(1)} dynamic-update-slice(f16[256,6144]{0,1:T(8,128)(2,1)S(1)} %dynamic_update_slice.48, f16[16,6144]{0,1:T(8,128)(2,1)} %copy.67, s32[]{:T(128)S(6)} %select_n.139, s32[]{:T(128)} %constant.124.clone.1) | dynamic-update-slice | bytes 393220 | tf_op jit(solution)/shard_map/dynamic_update_slice | solution.py:50
  125.2 17.0 %dynamic_update_slice.50 = f16[256,6144]{0,1:T(8,128)(2,1)S(1)} dynamic-update-slice(f16[256,6144]{0,1:T(8,128)(2,1)S(1)} %dynamic_update_slice.49, f16[16,6144]{0,1:T(8,128)(2,1)} %copy.68, s32[]{:T(128)S(6)} %select_n.141, s32[]{:T(128)} %constant.124.clone.1) | dynamic-update-slice | bytes 393220 | tf_op jit(solution)/shard_map/dynamic_update_slice | solution.py:53
  144.9 16.7 %dynamic_update_slice.51 = f16[256,6144]{0,1:T(8,128)(2,1)S(1)} dynamic-update-slice(f16[256,6144]{0,1:T(8,128)(2,1)S(1)} %dynamic_update_slice.50, f16[16,6144]{0,1:T(8,128)(2,1)} %copy.69, s32[]{:T(128)S(6)} %select_n.143, s32[]{:T(128)} %constant.124.clone.1) | dynamic-update-slice | bytes 393220 | tf_op jit(solution)/shard_map/dynamic_update_slice | solution.py:50
  164.4 17.0 %dynamic_update_slice.52 = f16[256,6144]{0,1:T(8,128)(2,1)S(1)} dynamic-update-slice(f16[256,6144]{0,1:T(8,128)(2,1)S(1)} %dynamic_update_slice.51, f16[16,6144]{0,1:T(8,128)(2,1)} %copy.70, s32[]{:T(128)S(6)} %select_n.145, s32[]{:T(128)} %constant.124.clone.1) | dynamic-update-slice | bytes 393220 | tf_op jit(solution)/shard_map/dynamic_update_slice | solution.py:53
  184.2 16.7 %dynamic_update_slice.53 = f16[256,6144]{0,1:T(8,128)(2,1)S(1)} dynamic-update-slice(f16[256,6144]{0,1:T(8,128)(2,1)S(1)} %dynamic_update_slice.52, f16[16,6144]{0,1:T(8,128)(2,1)} %copy.71, s32[]{:T(128)S(6)} %select_n.147, s32[]{:T(128)} %constant.124.clone.1) | dynamic-update-slice | bytes 393220 | tf_op jit(solution)/shard_map/dynamic_update_slice | solution.py:50
  203.6 17.0 %dynamic_update_slice.54 = f16[256,6144]{0,1:T(8,128)(2,1)S(1)} dynamic-update-slice(f16[256,6144]{0,1:T(8,128)(2,1)S(1)} %dynamic_update_slice.53, f16[16,6144]{0,1:T(8,128)(2,1)} %copy.72, s32[]{:T(128)S(6)} %select_n.149, s32[]{:T(128)} %constant.124.clone.1) | dynamic-update-slice | bytes 393220 | tf_op jit(solution)/shard_map/dynamic_update_slice | solution.py:53
  223.4 16.7 %dynamic_update_slice.55 = f16[256,6144]{0,1:T(8,128)(2,1)S(1)} dynamic-update-slice(f16[256,6144]{0,1:T(8,128)(2,1)S(1)} %dynamic_update_slice.54, f16[16,6144]{0,1:T(8,128)(2,1)} %copy.73, s32[]{:T(128)S(6)} %select_n.151, s32[]{:T(128)} %constant.124.clone.1) | dynamic-update-slice | bytes 393220 | tf_op jit(solution)/shard_map/dynamic_update_slice | solution.py:50
  242.9 17.0 %dynamic_update_slice.56 = f16[256,6144]{0,1:T(8,128)(2,1)S(1)} dynamic-update-slice(f16[256,6144]{0,1:T(8,128)(2,1)S(1)} %dynamic_update_slice.55, f16[16,6144]{0,1:T(8,128)(2,1)} %copy.74, s32[]{:T(128)S(6)} %select_n.153, s32[]{:T(128)} %constant.124.clone.1) | dynamic-update-slice | bytes 393220 | tf_op jit(solution)/shard_map/dynamic_update_slice | solution.py:53
  262.6 16.7 %dynamic_update_slice.57 = f16[256,6144]{0,1:T(8,128)(2,1)S(1)} dynamic-update-slice(f16[256,6144]{0,1:T(8,128)(2,1)S(1)} %dynamic_update_slice.56, f16[16,6144]{0,1:T(8,128)(2,1)} %copy.75, s32[]{:T(128)S(6)} %select_n.155, s32[]{:T(128)} %constant.124.clone.1) | dynamic-update-slice | bytes 393220 | tf_op jit(solution)/shard_map/dynamic_update_slice | solution.py:50
  282.1 17.0 %dynamic_update_slice.58 = f16[256,6144]{0,1:T(8,128)(2,1)S(1)} dynamic-update-slice(f16[256,6144]{0,1:T(8,128)(2,1)S(1)} %dynamic_update_slice.57, f16[16,6144]{0,1:T(8,128)(2,1)} %copy.76, s32[]{:T(128)S(6)} %select_n.157, s32[]{:T(128)} %constant.124.clone.1) | dynamic-update-slice | bytes 393220 | tf_op jit(solution)/shard_map/dynamic_update_slice | solution.py:53
  301.8 16.7 %dynamic_update_slice.59 = f16[256,6144]{0,1:T(8,128)(2,1)S(1)} dynamic-update-slice(f16[256,6144]{0,1:T(8,128)(2,1)S(1)} %dynamic_update_slice.58, f16[16,6144]{0,1:T(8,128)(2,1)} %copy.77, s32[]{:T(128)S(6)} %select_n.159, s32[]{:T(128)} %constant.124.clone.1) | dynamic-update-slice | bytes 393220 | tf_op jit(solution)/shard_map/dynamic_update_slice | solution.py:50
  321.3 17.0 %dynamic_update_slice.60 = f16[256,6144]{0,1:T(8,128)(2,1)S(1)} dynamic-update-slice(f16[256,6144]{0,1:T(8,128)(2,1)S(1)} %dynamic_update_slice.59, f16[16,6144]{0,1:T(8,128)(2,1)} %copy.78, s32[]{:T(128)S(6)} %select_n.161, s32[]{:T(128)} %constant.124.clone.1) | dynamic-update-slice | bytes 393220 | tf_op jit(solution)/shard_map/dynamic_update_slice | solution.py:53
  340.2 16.7 %dynamic_update_slice.61 = f16[256,6144]{0,1:T(8,128)(2,1)S(1)} dynamic-update-slice(f16[256,6144]{0,1:T(8,128)(2,1)S(1)} %dynamic_update_slice.60, f16[16,6144]{0,1:T(8,128)(2,1)} %copy.79, s32[]{:T(128)S(6)} %select_n.163, s32[]{:T(128)} %constant.124.clone.1) | dynamic-update-slice | bytes 393220 | tf_op jit(solution)/shard_map/dynamic_update_slice | solution.py:50
  359.7 17.0 %dynamic_update_slice.62 = f16[256,6144]{0,1:T(8,128)(2,1)S(1)} dynamic-update-slice(f16[256,6144]{0,1:T(8,128)(2,1)S(1)} %dynamic_update_slice.61, f16[16,6144]{0,1:T(8,128)(2,1)} %copy.80, s32[]{:T(128)S(6)} %select_n.165, s32[]{:T(128)} %constant.124.clone.1) | dynamic-update-slice | bytes 393220 | tf_op jit(solution)/shard_map/dynamic_update_slice | solution.py:53
  379.4 14.0 %dynamic_update_slice.63 = f16[256,6144]{0,1:T(8,128)(2,1)S(1)} dynamic-update-slice(f16[256,6144]{0,1:T(8,128)(2,1)S(1)} %dynamic_update_slice.62, f16[16,6144]{0,1:T(8,128)(2,1)} %copy.81, s32[]{:T(128)S(6)} %select_n.167, s32[]{:T(128)} %constant.124.clone.1) | dynamic-update-slice | bytes 393220 | tf_op jit(solution)/shard_map/dynamic_update_slice | solution.py:50
  396.8 7.4 %all-to-all-start.1 = ((bf16[32,48,256]{2,1,0:T(8,128)(2,1)}), bf16[32,48,256]{2,1,0:T(8,128)(2,1)}, u32[]{:S(2)}, u32[]{:S(2)}) async-start(bf16[32,48,256]{2,1,0:T(8,128)(2,1)} %bitcast.42), calls=%async_computation.1 | async-start | bytes 1572864 | tf_op jit(solution)/shard_map/all_to_all | solution.py:75
  405.9 12.6 %all-to-all-done.1 = bf16[32,48,256]{2,1,0:T(8,128)(2,1)} async-done(((bf16[32,48,256]{2,1,0:T(8,128)(2,1)}), bf16[32,48,256]{2,1,0:T(8,128)(2,1)}, u32[]{:S(2)}, u32[]{:S(2)}) %all-to-all-start.1) | async-done | bytes 786464 | tf_op jit(solution)/shard_map/all_to_all | solution.py:75
  (91 shorter events, 94.2 us)
Async XLA Ops:
  3.4 16.6 %collective-permute-start = (f16[16,6144]{1,0:T(8,128)(2,1)S(1)}, f16[16,6144]{1,0:T(8,128)(2,1)S(1)}, u32[]{:S(2)}, u32[]{:S(2)}) collective-permute-start(f16[16,6144]{1,0:T(8,128)(2,1)S(1)} %pad_maximum_fusion), channel_id=1, source_target_pairs={{0,32},{32,64},{64,96},{96,128},{128,160},{160,192},{192,224},{224... | collective-permute-start | bytes 589832 | tf_op jit(solution)/shard_map/ppermute | solution.py:49
  7.8 14.1 %collective-permute-start.1 = (f16[16,6144]{1,0:T(8,128)(2,1)S(1)}, f16[16,6144]{1,0:T(8,128)(2,1)S(1)}, u32[]{:S(2)}, u32[]{:S(2)}) collective-permute-start(f16[16,6144]{1,0:T(8,128)(2,1)S(1)} %pad_maximum_fusion), channel_id=1, source_target_pairs={{0,480},{32,0},{64,32},{96,64},{128,96},{160,128},{192,160},{224,1... | collective-permute-start | bytes 589832 | tf_op jit(solution)/shard_map/ppermute | solution.py:52
  20.0 68.2 %copy-start.2 = (f16[16,6144]{1,0:T(8,128)(2,1)}, f16[16,6144]{1,0:T(8,128)(2,1)S(1)}, u32[]{:S(2)}) copy-start(f16[16,6144]{1,0:T(8,128)(2,1)S(1)} %collective-permute-done) | copy-start | bytes 589828
  20.0 8.3 %collective-permute-start.2 = (f16[16,6144]{1,0:T(8,128)(2,1)S(1)}, f16[16,6144]{1,0:T(8,128)(2,1)S(1)}, u32[]{:S(2)}, u32[]{:S(2)}) collective-permute-start(f16[16,6144]{1,0:T(8,128)(2,1)S(1)} %collective-permute-done), channel_id=1, source_target_pairs={{0,32},{32,64},{64,96},{96,128},{128,160},{160,192},{192,224},{224... | collective-permute-start | bytes 589832 | tf_op jit(solution)/shard_map/ppermute | solution.py:49
  21.9 66.3 %copy-start = (f16[16,6144]{1,0:T(8,128)(2,1)}, f16[16,6144]{1,0:T(8,128)(2,1)S(1)}, u32[]{:S(2)}) copy-start(f16[16,6144]{1,0:T(8,128)(2,1)S(1)} %collective-permute-done.1) | copy-start | bytes 589828
  21.9 8.2 %collective-permute-start.3 = (f16[16,6144]{1,0:T(8,128)(2,1)S(1)}, f16[16,6144]{1,0:T(8,128)(2,1)S(1)}, u32[]{:S(2)}, u32[]{:S(2)}) collective-permute-start(f16[16,6144]{1,0:T(8,128)(2,1)S(1)} %collective-permute-done.1), channel_id=1, source_target_pairs={{0,480},{32,0},{64,32},{96,64},{128,96},{160,128},{192,160},{224,1... | collective-permute-start | bytes 589832 | tf_op jit(solution)/shard_map/ppermute | solution.py:52
  28.2 60.0 %copy-start.1 = (f16[16,6144]{1,0:T(8,128)(2,1)}, f16[16,6144]{1,0:T(8,128)(2,1)S(1)}, u32[]{:S(2)}) copy-start(f16[16,6144]{1,0:T(8,128)(2,1)S(1)} %collective-permute-done.2) | copy-start | bytes 589828
  28.2 7.6 %collective-permute-start.4 = (f16[16,6144]{1,0:T(8,128)(2,1)S(1)}, f16[16,6144]{1,0:T(8,128)(2,1)S(1)}, u32[]{:S(2)}, u32[]{:S(2)}) collective-permute-start(f16[16,6144]{1,0:T(8,128)(2,1)S(1)} %collective-permute-done.2), channel_id=1, source_target_pairs={{0,32},{32,64},{64,96},{96,128},{128,160},{160,192},{192,224},{224... | collective-permute-start | bytes 589832 | tf_op jit(solution)/shard_map/ppermute | solution.py:49
  30.1 58.0 %copy-start.3 = (f16[16,6144]{1,0:T(8,128)(2,1)}, f16[16,6144]{1,0:T(8,128)(2,1)S(1)}, u32[]{:S(2)}) copy-start(f16[16,6144]{1,0:T(8,128)(2,1)S(1)} %collective-permute-done.3) | copy-start | bytes 589828
  30.2 7.6 %collective-permute-start.5 = (f16[16,6144]{1,0:T(8,128)(2,1)S(1)}, f16[16,6144]{1,0:T(8,128)(2,1)S(1)}, u32[]{:S(2)}, u32[]{:S(2)}) collective-permute-start(f16[16,6144]{1,0:T(8,128)(2,1)S(1)} %collective-permute-done.3), channel_id=1, source_target_pairs={{0,480},{32,0},{64,32},{96,64},{128,96},{160,128},{192,160},{224,1... | collective-permute-start | bytes 589832 | tf_op jit(solution)/shard_map/ppermute | solution.py:52
  35.8 52.4 %copy-start.4 = (f16[16,6144]{1,0:T(8,128)(2,1)}, f16[16,6144]{1,0:T(8,128)(2,1)S(1)}, u32[]{:S(2)}) copy-start(f16[16,6144]{1,0:T(8,128)(2,1)S(1)} %collective-permute-done.4) | copy-start | bytes 589828
  35.8 7.6 %collective-permute-start.6 = (f16[16,6144]{1,0:T(8,128)(2,1)S(1)}, f16[16,6144]{1,0:T(8,128)(2,1)S(1)}, u32[]{:S(2)}, u32[]{:S(2)}) collective-permute-start(f16[16,6144]{1,0:T(8,128)(2,1)S(1)} %collective-permute-done.4), channel_id=1, source_target_pairs={{0,32},{32,64},{64,96},{96,128},{128,160},{160,192},{192,224},{224... | collective-permute-start | bytes 589832 | tf_op jit(solution)/shard_map/ppermute | solution.py:49
  37.8 50.4 %copy-start.5 = (f16[16,6144]{1,0:T(8,128)(2,1)}, f16[16,6144]{1,0:T(8,128)(2,1)S(1)}, u32[]{:S(2)}) copy-start(f16[16,6144]{1,0:T(8,128)(2,1)S(1)} %collective-permute-done.5) | copy-start | bytes 589828
  37.8 7.6 %collective-permute-start.7 = (f16[16,6144]{1,0:T(8,128)(2,1)S(1)}, f16[16,6144]{1,0:T(8,128)(2,1)S(1)}, u32[]{:S(2)}, u32[]{:S(2)}) collective-permute-start(f16[16,6144]{1,0:T(8,128)(2,1)S(1)} %collective-permute-done.5), channel_id=1, source_target_pairs={{0,480},{32,0},{64,32},{96,64},{128,96},{160,128},{192,160},{224,1... | collective-permute-start | bytes 589832 | tf_op jit(solution)/shard_map/ppermute | solution.py:52
  43.4 44.8 %copy-start.6 = (f16[16,6144]{1,0:T(8,128)(2,1)}, f16[16,6144]{1,0:T(8,128)(2,1)S(1)}, u32[]{:S(2)}) copy-start(f16[16,6144]{1,0:T(8,128)(2,1)S(1)} %collective-permute-done.6) | copy-start | bytes 589828
  43.5 7.6 %collective-permute-start.8 = (f16[16,6144]{1,0:T(8,128)(2,1)S(1)}, f16[16,6144]{1,0:T(8,128)(2,1)S(1)}, u32[]{:S(2)}, u32[]{:S(2)}) collective-permute-start(f16[16,6144]{1,0:T(8,128)(2,1)S(1)} %collective-permute-done.6), channel_id=1, source_target_pairs={{0,32},{32,64},{64,96},{96,128},{128,160},{160,192},{192,224},{224... | collective-permute-start | bytes 589832 | tf_op jit(solution)/shard_map/ppermute | solution.py:49
  45.4 7.6 %collective-permute-start.9 = (f16[16,6144]{1,0:T(8,128)(2,1)S(1)}, f16[16,6144]{1,0:T(8,128)(2,1)S(1)}, u32[]{:S(2)}, u32[]{:S(2)}) collective-permute-start(f16[16,6144]{1,0:T(8,128)(2,1)S(1)} %collective-permute-done.7), channel_id=1, source_target_pairs={{0,480},{32,0},{64,32},{96,64},{128,96},{160,128},{192,160},{224,1... | collective-permute-start | bytes 589832 | tf_op jit(solution)/shard_map/ppermute | solution.py:52
  51.1 7.6 %collective-permute-start.10 = (f16[16,6144]{1,0:T(8,128)(2,1)S(1)}, f16[16,6144]{1,0:T(8,128)(2,1)S(1)}, u32[]{:S(2)}, u32[]{:S(2)}) collective-permute-start(f16[16,6144]{1,0:T(8,128)(2,1)S(1)} %collective-permute-done.8), channel_id=1, source_target_pairs={{0,32},{32,64},{64,96},{96,128},{128,160},{160,192},{192,224},{224... | collective-permute-start | bytes 589832 | tf_op jit(solution)/shard_map/ppermute | solution.py:49
  53.0 9.1 %collective-permute-start.11 = (f16[16,6144]{1,0:T(8,128)(2,1)S(1)}, f16[16,6144]{1,0:T(8,128)(2,1)}, u32[]{:S(2)}, u32[]{:S(2)}) collective-permute-start(f16[16,6144]{1,0:T(8,128)(2,1)S(1)} %collective-permute-done.9), channel_id=1, source_target_pairs={{0,480},{32,0},{64,32},{96,64},{128,96},{160,128},{192,160},{224,1... | collective-permute-start | bytes 589832 | tf_op jit(solution)/shard_map/ppermute | solution.py:52
  58.7 8.2 %collective-permute-start.12 = (f16[16,6144]{1,0:T(8,128)(2,1)S(1)}, f16[16,6144]{1,0:T(8,128)(2,1)S(1)}, u32[]{:S(2)}, u32[]{:S(2)}) collective-permute-start(f16[16,6144]{1,0:T(8,128)(2,1)S(1)} %collective-permute-done.10), channel_id=1, source_target_pairs={{0,32},{32,64},{64,96},{96,128},{128,160},{160,192},{192,224},{224... | collective-permute-start | bytes 589832 | tf_op jit(solution)/shard_map/ppermute | solution.py:49
  62.1 294.8 %collective-permute-start.13 = (f16[16,6144]{1,0:T(8,128)(2,1)}, f16[16,6144]{1,0:T(8,128)(2,1)}, u32[]{:S(2)}, u32[]{:S(2)}) collective-permute-start(f16[16,6144]{1,0:T(8,128)(2,1)} %collective-permute-done.11), channel_id=1, source_target_pairs={{0,480},{32,0},{64,32},{96,64},{128,96},{160,128},{192,160},{224,1... | collective-permute-start | bytes 589832 | tf_op jit(solution)/shard_map/ppermute | solution.py:52
  66.8 309.8 %collective-permute-start.14 = (f16[16,6144]{1,0:T(8,128)(2,1)S(1)}, f16[16,6144]{1,0:T(8,128)(2,1)}, u32[]{:S(2)}, u32[]{:S(2)}) collective-permute-start(f16[16,6144]{1,0:T(8,128)(2,1)S(1)} %collective-permute-done.12), channel_id=1, source_target_pairs={{0,32},{32,64},{64,96},{96,128},{128,160},{160,192},{192,224},{224... | collective-permute-start | bytes 589832 | tf_op jit(solution)/shard_map/ppermute | solution.py:49
  69.6 33.2 %all-to-all-start = ((s32[32,1,128]{2,1,0:T(1,128)}), s32[32,1,128]{2,1,0:T(1,128)S(1)}, u32[]{:S(2)}, u32[]{:S(2)}) async-start(s32[32,1,128]{2,1,0:T(1,128)} %bitcast.4), calls=%async_computation | async-start | bytes 32768 | tf_op jit(solution)/shard_map/all_to_all | solution.py:32
  396.8 21.7 %all-to-all-start.1 = ((bf16[32,48,256]{2,1,0:T(8,128)(2,1)}), bf16[32,48,256]{2,1,0:T(8,128)(2,1)}, u32[]{:S(2)}, u32[]{:S(2)}) async-start(bf16[32,48,256]{2,1,0:T(8,128)(2,1)} %bitcast.42), calls=%async_computation.1 | async-start | bytes 1572864 | tf_op jit(solution)/shard_map/all_to_all | solution.py:75
  (5 other events, 159.1 us)
